TPU v7x, 256 devices: a whole 4x4x8 slice. The times are simulated.
256 devices in a mesh: req: 16 (over z, core), mp: 16 (over x, y).
Axes of the slice: x: 4, y: 4, z: 8, core: 2. Of those that a mesh axis runs over, the one named last changes fastest.
Arguments:
- tokens_in: bfloat16 [2048, 2048], P('req', 'mp'), may hold values from -6 to 6
- req_lengths: int32 [16, 4], replicated, may hold values from 1 to 64, 128 in all within a row
- req_groups: int32 [16, 4], replicated, may hold values from 0 to 1
- prefix_cache: bfloat16 [2, 4096, 2, 2048], P(None, 'req', None, 'mp'), may hold values from -170 to 170, as said below
- attn_gain: bfloat16 [2048], replicated, may hold values from 0.25 to 1.75
- mlp_gain: bfloat16 [2048], replicated, may hold values from 0.25 to 1.75
- w_qkv: bfloat16 [2048, 3, 2048], P(None, None, 'mp'), may hold values from -0.25 to 0.25
- w_out: bfloat16 [2048, 2048], P('mp'), may hold values from -0.1875 to 0.1875
- w_gate_up: bfloat16 [2048, 2, 5632], P(None, None, 'mp'), may hold values from -0.125 to 0.125
- w_down: bfloat16 [5632, 2048], P('mp'), may hold values from -0.109375 to 0.109375
Outputs:
- layer_out: bfloat16 [2048, 2048], P('req', 'mp')
Inputs may be any that keep to these rules, and one draw needn't show every extreme that they name: `req_lengths`: in each row the 4 lengths sum to 128, and the largest is 64. `prefix_cache`: keys are cached after rotation.
All inputs are finite; a program needn't handle non-finite values.
Results may differ from a plain program's by a relative error of at most 0.02.
The roundings to bfloat16 on the way count: a program that leaves them out, or rounds other values in their place, can miss the bound.
Values may be sent and summed in bfloat16 or wider, within the bound.
A program may use at most 64 MiB of HBM per device.

v0:
```python
import jax
import jax.numpy as jnp
from jax import lax
from jax.sharding import PartitionSpec as P

HEAD_DIM = 64
ROT = 16
PREFIX = 4096
GROUPS = 2
NEG = -1e30
EPS = 1e-05


def layer_norm(rows_in, gain_vec):
    values_f = rows_in.astype(jnp.float32)
    row_mean = jnp.mean(values_f, axis=-1, keepdims=True)
    centred = values_f - row_mean
    variance = jnp.mean(centred * centred, axis=-1, keepdims=True)
    return (centred * lax.rsqrt(variance + EPS) * gain_vec.astype(jnp.float32)).astype(jnp.bfloat16)


def rotary(vectors, positions):
    half_rot = ROT // 2
    frequency = 10000.0 ** (-(jnp.arange(half_rot, dtype=jnp.float32) * 2.0 / ROT))
    angles = positions[:, None] * frequency[None, :]
    cosine = jnp.cos(angles)[:, None, :]
    sine_part = jnp.sin(angles)[:, None, :]
    lower_half = vectors[..., :half_rot]
    upper_half = vectors[..., half_rot:ROT]
    return jnp.concatenate(
        [
            lower_half * cosine - upper_half * sine_part,
            upper_half * cosine + lower_half * sine_part,
            vectors[..., ROT:],
        ],
        axis=-1,
    )


def token_meta(length_row, group_row, row_count):
    starts = jnp.cumsum(length_row) - length_row
    places = jnp.arange(row_count, dtype=jnp.int32)
    request = jnp.sum((places[:, None] >= starts[None, :]).astype(jnp.int32), axis=1) - 1
    onehot = (request[:, None] == jnp.arange(length_row.shape[0], dtype=jnp.int32)[None, :]).astype(
        jnp.int32
    )
    offset = places - jnp.sum(onehot * starts[None, :], axis=1)
    groups_of = jnp.sum(onehot * group_row[None, :], axis=1)
    return (request, offset, groups_of)


def combine_states(state_a, state_b):
    mixed_a, top_a, sum_a = state_a
    mixed_b, top_b, sum_b = state_b
    top_new = jnp.maximum(top_a, top_b)
    scale_a = jnp.exp(top_a - top_new)
    scale_b = jnp.exp(top_b - top_new)
    return (
        mixed_a * scale_a[..., None] + mixed_b * scale_b[..., None],
        top_new,
        sum_a * scale_a + sum_b * scale_b,
    )


def rounded_block(query, member, part):
    group_count = part.shape[0]
    block = part.shape[1]
    row_count = query.shape[0]
    heads = query.shape[1]
    key_part = part[:, :, 0].reshape(group_count, block, heads, HEAD_DIM)
    value_part = part[:, :, 1].reshape(group_count * block, heads, HEAD_DIM)
    scores = jnp.einsum(
        "thd,gnhd->htgn", query, key_part, preferred_element_type=jnp.float32
    ) * HEAD_DIM ** (-0.5)
    scores = jnp.where(member[None, :, :, None], scores, NEG).reshape(
        heads, row_count, group_count * block
    )
    top_score = jnp.max(scores, axis=2)
    weights = jnp.exp(scores - top_score[:, :, None])
    weight_sum = jnp.sum(weights, axis=2)
    mixed_out = jnp.einsum(
        "hts,she->the", weights.astype(jnp.bfloat16), value_part, preferred_element_type=jnp.float32
    )
    normed_part = (mixed_out / weight_sum.T[..., None]).astype(jnp.bfloat16)
    return (normed_part, top_score.T, weight_sum.T)


def own_attention(query, keys, values, request, offset):
    scores = jnp.einsum(
        "thd,shd->hts", query, keys, preferred_element_type=jnp.float32
    ) * HEAD_DIM ** (-0.5)
    allowed = (request[:, None] == request[None, :]) & (offset[None, :] <= offset[:, None])
    scores = jnp.where(allowed[None], scores, NEG)
    top_score = jnp.max(scores, axis=2)
    weights = jnp.exp(scores - top_score[:, :, None])
    weight_sum = jnp.sum(weights, axis=2)
    mixed_out = jnp.einsum(
        "hts,she->the", weights.astype(jnp.bfloat16), values, preferred_element_type=jnp.float32
    )
    return (mixed_out, top_score.T, weight_sum.T)


def body(
    tokens_in,
    req_lengths,
    req_groups,
    prefix_cache,
    attn_gain,
    mlp_gain,
    w_qkv,
    w_out,
    w_gate_up,
    w_down,
):
    row_count = tokens_in.shape[0]
    shard_width = tokens_in.shape[1]
    device_row = lax.axis_index("req")
    mp_index = lax.axis_index("mp")
    full_rows = lax.all_gather(tokens_in, "mp", axis=1, tiled=True)
    model_width = full_rows.shape[1]
    normed_attn = layer_norm(full_rows, attn_gain)
    heads = w_qkv.shape[2] // HEAD_DIM
    projected = jnp.dot(
        normed_attn, w_qkv.reshape(model_width, -1), preferred_element_type=jnp.float32
    )
    projected = projected.reshape(row_count, 3, heads, HEAD_DIM)
    length_row = lax.dynamic_index_in_dim(req_lengths, device_row, 0, keepdims=False)
    group_row = lax.dynamic_index_in_dim(req_groups, device_row, 0, keepdims=False)
    request, offset, groups_of = token_meta(length_row, group_row, row_count)
    positions = (PREFIX + offset).astype(jnp.float32)
    query_rot = rotary(projected[:, 0], positions).astype(jnp.bfloat16)
    key_rot = rotary(projected[:, 1], positions).astype(jnp.bfloat16)
    value_rows = projected[:, 2].astype(jnp.bfloat16)
    own_state = own_attention(query_rot, key_rot, value_rows, request, offset)
    group_ids = jnp.arange(GROUPS, dtype=jnp.int32)
    block_rows = prefix_cache.shape[1]
    member = groups_of[:, None] == group_ids[None, :]
    piece = lax.all_gather(prefix_cache, "req", axis=1, tiled=True)

    def step_block(index, carry):
        part = lax.dynamic_slice_in_dim(piece, index * block_rows, block_rows, 1)
        normed_part, part_top, part_sum = rounded_block(query_rot, member, part)
        return combine_states(
            carry, (normed_part.astype(jnp.float32) * part_sum[..., None], part_top, part_sum)
        )

    mixed_out, top_score, weight_sum = lax.fori_loop(
        0, piece.shape[1] // block_rows, step_block, own_state
    )
    attn_rows = (
        (mixed_out / weight_sum[..., None])
        .astype(jnp.bfloat16)
        .reshape(row_count, heads * HEAD_DIM)
    )
    attn_part = jnp.dot(attn_rows, w_out, preferred_element_type=jnp.float32)
    attn_share = lax.psum_scatter(
        attn_part.astype(jnp.bfloat16), "mp", scatter_dimension=1, tiled=True
    ).astype(jnp.float32)
    residual_share = (tokens_in.astype(jnp.float32) + attn_share).astype(jnp.bfloat16)
    residual_f = residual_share.astype(jnp.float32)
    row_sums, row_squares = lax.psum(
        (jnp.sum(residual_f, axis=1), jnp.sum(residual_f * residual_f, axis=1)), "mp"
    )
    row_mean = row_sums / model_width
    variance = row_squares / model_width - row_mean * row_mean
    gain_share = lax.dynamic_slice_in_dim(mlp_gain, mp_index * shard_width, shard_width, 0).astype(
        jnp.float32
    )
    normed_share = (
        (residual_f - row_mean[:, None]) * lax.rsqrt(variance + EPS)[:, None] * gain_share[None, :]
    ).astype(jnp.bfloat16)
    normed_mlp = lax.all_gather(normed_share, "mp", axis=1, tiled=True)
    local_units = w_gate_up.shape[2]
    gate_up = jnp.dot(
        normed_mlp, w_gate_up.reshape(model_width, -1), preferred_element_type=jnp.float32
    ).reshape(row_count, 2, local_units)
    hidden = (jax.nn.silu(gate_up[:, 0]) * gate_up[:, 1]).astype(jnp.bfloat16)
    down_part = jnp.dot(hidden, w_down, preferred_element_type=jnp.float32)
    mlp_share = lax.psum_scatter(
        down_part.astype(jnp.bfloat16), "mp", scatter_dimension=1, tiled=True
    ).astype(jnp.float32)
    return (residual_share.astype(jnp.float32) + mlp_share).astype(jnp.bfloat16)


def solution(mesh):
    return jax.shard_map(
        body,
        mesh=mesh,
        in_specs=(
            P("req", "mp"),
            P(),
            P(),
            P(None, "req", None, "mp"),
            P(),
            P(),
            P(None, None, "mp"),
            P("mp", None),
            P(None, None, "mp"),
            P("mp", None),
        ),
        out_specs=P("req", "mp"),
        check_vma=False,
    )
```

profile of v0, /device:TPU:2, one launch (start us, length us, event | category | flops | bytes accessed | tf_op | source)
XLA Modules:
  0.0 390.6 jit_solution(3455351838395979648)
XLA Ops:
  6.5 2.0 copy.31
  8.6 2.6 copy.29
  11.2 24.8 %all_gather.9 = bf16[128,2048]{1,0:T(8,128)(2,1)S(1)} all-gather(bf16[128,128]{1,0:T(8,128)(2,1)S(1)} %copy-done.3), channel_id=1, replica_groups=mesh['req'=16,'mp'=16] {'mp'}, dimensions={1}, use_global_device_ids=true | all-gather | bytes 557056 | tf_op jit(solution)/shard_map/all_gather | solution.py:119
  39.7 21.0 %all-gather.2.cloned.1.call-done = bf16[2,4096,2,128]{1,3,0,2:T(8,128)(2,1)} async-done(((bf16[2,256,2,128]{1,3,0,2:T(8,128)(2,1)}), bf16[2,4096,2,128]{1,3,0,2:T(8,128)(2,1)}) %all-gather.2.cloned.1.call-update) | async-done | bytes 4194320 | tf_op jit(solution)/shard_map/all_gather | solution.py:138
  60.7 98.9 %while.18 = (s32[]{:T(128)}, f32[128,2,64]{0,2,1:T(8,128)}, f32[128,2]{0,1:T(2,128)S(1)}, f32[128,2]{0,1:T(2,128)S(1)}, bf16[2,4096,2,128]{1,3,0,2:T(8,128)(2,1)...) while((s32[]{:T(128)}, f32[128,2,64]{0,2,1:T(8,128)}, ...), condition=%wide.region_11.12_spmd.clone, body=%wide.region_8.11_spmd.clone.sunk | while | flops 34587912 | bytes 4112575 | solution.py:147
  60.7 1.6 constant_dynamic-slice_fusion.4
  64.9 2.0 fusion.64
  66.9 1.6 constant_dynamic-slice_fusion.4
  71.0 2.0 fusion.64
  77.2 2.0 fusion.64
  79.2 1.6 constant_dynamic-slice_fusion.4
  83.4 2.0 fusion.64
  89.6 2.0 fusion.64
  95.8 2.0 fusion.64
  97.8 1.6 constant_dynamic-slice_fusion.4
  102.0 2.0 fusion.64
  108.1 2.0 fusion.64
  114.3 2.0 fusion.64
  116.3 1.6 constant_dynamic-slice_fusion.4
  120.5 2.0 fusion.64
  126.7 2.0 fusion.64
  128.7 1.6 constant_dynamic-slice_fusion.4
  132.9 2.0 fusion.64
  139.0 2.0 fusion.64
  145.2 2.0 fusion.64
  147.2 1.6 constant_dynamic-slice_fusion.4
  151.4 2.0 fusion.64
  157.6 2.0 fusion.64
  163.6 76.5 %reduce-scatter.7.cloned.1.call-done = bf16[128,128]{1,0:T(8,128)(2,1)} async-done(((bf16[2048,128]{1,0:T(8,128)(2,1)}), bf16[128,128]{1,0:T(8,128)(2,1)}) %reduce-scatter.7.cloned.1.call-update) | async-done | bytes 32784
  241.1 33.3 %all-reduce = (f32[128]{0:T(128)S(1)}, f32[128]{0:T(128)S(1)}) all-reduce(f32[128]{0:T(128)S(1)} %get-tuple-element.150, f32[128]{0:T(128)S(1)} %get-tuple-element.149), channel_id=1, replica_groups=mesh['req'=16,'mp'=16] {'mp'}, use_global_device_ids=true, to_apply=%region_16.17 | all-reduce | flops 256 | bytes 2048 | tf_op jit(solution)/shard_map/psum | solution.py:161
  274.5 27.3 %all_gather.11 = bf16[128,2048]{1,0:T(8,128)(2,1)S(1)} all-gather(bf16[128,128]{1,0:T(8,128)(2,1)S(1)} %fusion.37), channel_id=1, replica_groups=mesh['req'=16,'mp'=16] {'mp'}, dimensions={1}, use_global_device_ids=true | all-gather | bytes 557056 | tf_op jit(solution)/shard_map/all_gather | solution.py:172
  304.8 77.8 %reduce-scatter.9.cloned.1.call-done = bf16[128,128]{1,0:T(8,128)(2,1)} async-done(((bf16[2048,128]{1,0:T(8,128)(2,1)}), bf16[128,128]{1,0:T(8,128)(2,1)}) %reduce-scatter.9.cloned.1.call-update) | async-done | bytes 32784
  (180 shorter events, 68.6 us)
Async XLA Ops:
  6.5 295.3 %copy-start = (bf16[2048,2,352]{0,2,1:T(8,128)(2,1)S(1)}, bf16[2048,2,352]{0,2,1:T(8,128)(2,1)}, u32[]{:S(2)}) copy-start(bf16[2048,2,352]{0,2,1:T(8,128)(2,1)} %param.20) | copy-start | bytes 8650756
  6.5 54.1 %all-gather.2.cloned.1.call-start = ((), (), s32[]{:S(2)}) async-start(), calls=%async_computation.2 | async-start | bytes 4456448 | tf_op jit(solution)/shard_map/all_gather | solution.py:138
  8.5 231.6 %reduce-scatter.7.cloned.1.call-start = ((), (), s32[]{:S(2)}) async-start(), calls=%async_computation.3 | async-start | bytes 557056
  8.6 2.6 copy-start.5
  8.6 2.6 copy-start.3
  11.2 25.2 %copy-start.1 = (bf16[2048,3,128]{0,2,1:T(8,128)(2,1)S(1)}, bf16[2048,3,128]{0,2,1:T(8,128)(2,1)}, u32[]{:S(2)}) copy-start(bf16[2048,3,128]{0,2,1:T(8,128)(2,1)} %copy.29) | copy-start | bytes 4718596
  36.5 0.7 copy-start.6
  36.5 0.7 copy-start.7
  159.6 81.4 %copy-start.4 = (bf16[128,128]{1,0:T(8,128)(2,1)S(1)}, bf16[128,128]{1,0:T(8,128)(2,1)}, u32[]{:S(2)}) copy-start(bf16[128,128]{1,0:T(8,128)(2,1)} %param.12) | copy-start | bytes 98308
  162.8 219.8 %reduce-scatter.9.cloned.1.call-start = ((), (), s32[]{:S(2)}) async-start(), calls=%async_computation.4 | async-start | bytes 557056
  301.9 1.4 copy-start.2
Sparse Core Ops, SparseCore 0:
  9.1 51.5 all-gather.1
  162.9 77.1 reduce-scatter.6
  304.9 77.6 reduce-scatter.8
where the time goes:
time: 392 us; the launch traced here: 391 us
  waiting for transfers between devices  175 us (45%)
  blocking collectives  85.4 us (22%)
  matrix products  55.5 us (14%)
  local copies, waits for them, and re-layouts  54.7 us (14%)
  between operations  13.3 us (3%)
  other arithmetic  6.08 us (2%)
    unnamed x5, waiting for transfers between devices  154 us
    psum x1, blocking collectives, body(): lax.psum((jnp.sum(residual_f, axis=1), jnp.sum(residual_f * residual_f, a...  33.3 us
    dot_general x16, matrix products, rounded_block(): jnp.einsum('hts,she->the', weights.astype(jnp.bfloat16), value_part, pref...  31.8 us
    all_gather x1, blocking collectives, body(): normed_mlp = lax.all_gather(normed_share, 'mp', axis=1, tiled=True)  27.3 us
    slice x16, local copies, waits for them, and re-layouts, rounded_block(): key_part = part[:, :, 0].reshape(group_count, block, heads, HEAD_DIM)  26.1 us
    all_gather x1, blocking collectives, body(): full_rows = lax.all_gather(tokens_in, 'mp', axis=1, tiled=True)  24.8 us
    all_gather x1, waiting for transfers between devices, body(): piece = lax.all_gather(prefix_cache, 'req', axis=1, tiled=True)  21 us
    dot_general x16, matrix products, rounded_block(): jnp.einsum('thd,gnhd->htgn', query, key_part, preferred_element_type=jnp....  19.2 us
  transfers between devices with their start and end apart: 3, of which 3 were waited for; matrix products, arithmetic and copies ran while one was open for 2% of the time, Pallas kernels for 0%

commit v1 on v0

--- a/solution.py
+++ b/solution.py
@@ -116,7 +116,25 @@
     shard_width = tokens_in.shape[1]
     device_row = lax.axis_index("req")
     mp_index = lax.axis_index("mp")
-    full_rows = lax.all_gather(tokens_in, "mp", axis=1, tiled=True)
+    size, position, span = (lax.axis_size("mp"), lax.axis_index("mp"), tokens_in.shape[1])
+    forward = [(i, (i + 1) % size) for i in range(size)]
+    downward = [(i, (i - 1) % size) for i in range(size)]
+    full_rows = jnp.zeros(
+        (*tokens_in.shape[:1], size * span, *tokens_in.shape[1 + 1 :]), tokens_in.dtype
+    )
+    full_rows = lax.dynamic_update_slice_in_dim(full_rows, tokens_in, position * span, axis=1)
+    from_left = from_right = tokens_in
+    half = size // 2
+    for step in range(1, half + 1):
+        from_left = lax.ppermute(from_left, "mp", forward)
+        full_rows = lax.dynamic_update_slice_in_dim(
+            full_rows, from_left, (position - step) % size * span, axis=1
+        )
+        if step < size - half:
+            from_right = lax.ppermute(from_right, "mp", downward)
+            full_rows = lax.dynamic_update_slice_in_dim(
+                full_rows, from_right, (position + step) % size * span, axis=1
+            )
     model_width = full_rows.shape[1]
     normed_attn = layer_norm(full_rows, attn_gain)
     heads = w_qkv.shape[2] // HEAD_DIM

time: 392 us -> 404 us (1.031)
  starting transfers between devices: 0.09 us -> 29.2 us
  blocking collectives: 85.4 us -> 60.6 us
  waiting for transfers between devices: 175 us -> 180 us
    ppermute x0 -> x15, starting transfers between devices: none -> 29.1 us  [the longest x7 27.3 us: body(): from_right = lax.ppermute(from_right, 'mp', downward)]
    all_gather x1 -> x0, blocking collectives: 24.8 us -> none  [body(): full_rows = lax.all_gather(tokens_in, 'mp', axis=1, tiled=True)]
    all_gather x1, waiting for transfers between devices: 21 us -> 0.01 us  [body(): piece = lax.all_gather(prefix_cache, 'req', axis=1, tiled=True)]
    ppermute x0 -> x15, waiting for transfers between devices: none -> 17.2 us  [the longest x8 17.2 us: body(): from_left = lax.ppermute(from_left, 'mp', forward)]
    unnamed x5, waiting for transfers between devices: 154 us -> 163 us
    unnamed x22 -> x16, local copies, waits for them, and re-layouts: 8.77 us -> 8.75 us
  transfers between devices with their start and end apart: 3 -> 18, of which waited for: 3 -> 9; matrix products, arithmetic and copies ran while one was open for 2% -> 2% of each run, Pallas kernels for 0% -> 0%
where the time goes in v1:
time: 404 us; the launch traced here: 403 us
  waiting for transfers between devices  180 us (45%)
  blocking collectives  60.6 us (15%)
  local copies, waits for them, and re-layouts  56.3 us (14%)
  matrix products  55.5 us (14%)
  starting transfers between devices  29.2 us (7%)
  between operations  13.4 us (3%)
  other arithmetic  6.89 us (2%)
    unnamed x5, waiting for transfers between devices  163 us
    psum x1, blocking collectives, body(): lax.psum((jnp.sum(residual_f, axis=1), jnp.sum(residual_f * residual_f, a...  33.3 us
    dot_general x16, matrix products, rounded_block(): jnp.einsum('hts,she->the', weights.astype(jnp.bfloat16), value_part, pref...  31.8 us
    ppermute x7, starting transfers between devices, body(): from_right = lax.ppermute(from_right, 'mp', downward)  27.3 us
    all_gather x1, blocking collectives, body(): normed_mlp = lax.all_gather(normed_share, 'mp', axis=1, tiled=True)  27.3 us
    slice x16, local copies, waits for them, and re-layouts, rounded_block(): key_part = part[:, :, 0].reshape(group_count, block, heads, HEAD_DIM)  26.1 us
    dot_general x16, matrix products, rounded_block(): jnp.einsum('thd,gnhd->htgn', query, key_part, preferred_element_type=jnp....  19.2 us
    ppermute x8, waiting for transfers between devices, body(): from_left = lax.ppermute(from_left, 'mp', forward)  17.2 us
  transfers between devices with their start and end apart: 18, of which 9 were waited for; matrix products, arithmetic and copies ran while one was open for 2% of the time, Pallas kernels for 0%

profile of v1, /device:TPU:2, one launch (start us, length us, event | category | flops | bytes accessed | tf_op | source)
XLA Modules:
  0.0 402.5 jit_solution(10997921958284131445)
XLA Ops:
  6.5 2.0 copy.31
  10.2 2.6 collective-permute-start.1
  15.8 2.6 copy.29
  18.5 4.1 %collective-permute-start.3 = (bf16[128,128]{1,0:T(8,128)(2,1)S(1)}, bf16[128,128]{1,0:T(8,128)(2,1)S(1)}, u32[]{:S(2)}, u32[]{:S(2)}) collective-permute-start(bf16[128,128]{1,0:T(8,128)(2,1)S(1)} %collective-permute-done.1), channel_id=1, source_target_pairs={{0,15},{1,0},{2,1},{3,2},{4,3},{5,4},{6,5},{7,6},{8,7},{9,8},{10,9... | collective-permute-start | bytes 98312 | tf_op jit(solution)/shard_map/ppermute | solution.py:134
  24.5 4.1 %collective-permute-start.5 = (bf16[128,128]{1,0:T(8,128)(2,1)S(1)}, bf16[128,128]{1,0:T(8,128)(2,1)S(1)}, u32[]{:S(2)}, u32[]{:S(2)}) collective-permute-start(bf16[128,128]{1,0:T(8,128)(2,1)S(1)} %collective-permute-done.3), channel_id=1, source_target_pairs={{0,15},{1,0},{2,1},{3,2},{4,3},{5,4},{6,5},{7,6},{8,7},{9,8},{10,9... | collective-permute-start | bytes 98312 | tf_op jit(solution)/shard_map/ppermute | solution.py:134
  30.6 4.1 %collective-permute-start.7 = (bf16[128,128]{1,0:T(8,128)(2,1)S(1)}, bf16[128,128]{1,0:T(8,128)(2,1)S(1)}, u32[]{:S(2)}, u32[]{:S(2)}) collective-permute-start(bf16[128,128]{1,0:T(8,128)(2,1)S(1)} %collective-permute-done.5), channel_id=1, source_target_pairs={{0,15},{1,0},{2,1},{3,2},{4,3},{5,4},{6,5},{7,6},{8,7},{9,8},{10,9... | collective-permute-start | bytes 98312 | tf_op jit(solution)/shard_map/ppermute | solution.py:134
  36.6 4.1 %collective-permute-start.9 = (bf16[128,128]{1,0:T(8,128)(2,1)S(1)}, bf16[128,128]{1,0:T(8,128)(2,1)S(1)}, u32[]{:S(2)}, u32[]{:S(2)}) collective-permute-start(bf16[128,128]{1,0:T(8,128)(2,1)S(1)} %collective-permute-done.7), channel_id=1, source_target_pairs={{0,15},{1,0},{2,1},{3,2},{4,3},{5,4},{6,5},{7,6},{8,7},{9,8},{10,9... | collective-permute-start | bytes 98312 | tf_op jit(solution)/shard_map/ppermute | solution.py:134
  40.8 1.9 collective-permute-done.8
  42.7 4.1 %collective-permute-start.11 = (bf16[128,128]{1,0:T(8,128)(2,1)S(1)}, bf16[128,128]{1,0:T(8,128)(2,1)S(1)}, u32[]{:S(2)}, u32[]{:S(2)}) collective-permute-start(bf16[128,128]{1,0:T(8,128)(2,1)S(1)} %collective-permute-done.9), channel_id=1, source_target_pairs={{0,15},{1,0},{2,1},{3,2},{4,3},{5,4},{6,5},{7,6},{8,7},{9,8},{10,9... | collective-permute-start | bytes 98312 | tf_op jit(solution)/shard_map/ppermute | solution.py:134
  48.7 4.1 %collective-permute-start.13 = (bf16[128,128]{1,0:T(8,128)(2,1)S(1)}, bf16[128,128]{1,0:T(8,128)(2,1)S(1)}, u32[]{:S(2)}, u32[]{:S(2)}) collective-permute-start(bf16[128,128]{1,0:T(8,128)(2,1)S(1)} %collective-permute-done.11), channel_id=1, source_target_pairs={{0,15},{1,0},{2,1},{3,2},{4,3},{5,4},{6,5},{7,6},{8,7},{9,8},{10,9... | collective-permute-start | bytes 98312 | tf_op jit(solution)/shard_map/ppermute | solution.py:134
  54.8 6.0 %collective-permute-done.14 = bf16[128,128]{1,0:T(8,128)(2,1)S(1)} collective-permute-done((bf16[128,128]{1,0:T(8,128)(2,1)S(1)}, bf16[128,128]{1,0:T(8,128)(2,1)S(1)}, u32[]{:S(2)}, u32[]{:S(2)}) %collective-permute-start.14) | collective-permute-done | bytes 32800 | tf_op jit(solution)/shard_map/ppermute | solution.py:129
  63.7 98.9 %while.18 = (s32[]{:T(128)}, f32[128,2,64]{0,2,1:T(8,128)}, f32[128,2]{0,1:T(2,128)S(1)}, f32[128,2]{0,1:T(2,128)S(1)}, bf16[2,4096,2,128]{1,3,0,2:T(8,128)(2,1)...) while((s32[]{:T(128)}, f32[128,2,64]{0,2,1:T(8,128)}, ...), condition=%wide.region_11.12_spmd.clone, body=%wide.region_8.11_spmd.clone.sunk | while | flops 34587912 | bytes 4112575 | solution.py:165
  67.8 2.0 fusion.65
  74.0 2.0 fusion.65
  80.2 2.0 fusion.65
  86.4 2.0 fusion.65
  92.6 2.0 fusion.65
  98.8 2.0 fusion.65
  104.9 2.0 fusion.65
  111.1 2.0 fusion.65
  117.3 2.0 fusion.65
  123.5 2.0 fusion.65
  129.7 2.0 fusion.65
  135.8 2.0 fusion.65
  142.0 2.0 fusion.65
  148.2 2.0 fusion.65
  154.4 2.0 fusion.65
  160.6 2.0 fusion.65
  166.6 85.4 %reduce-scatter.7.cloned.1.call-done = bf16[128,128]{1,0:T(8,128)(2,1)} async-done(((bf16[2048,128]{1,0:T(8,128)(2,1)}), bf16[128,128]{1,0:T(8,128)(2,1)}) %reduce-scatter.7.cloned.1.call-update) | async-done | bytes 32784
  253.0 33.3 %all-reduce = (f32[128]{0:T(128)S(1)}, f32[128]{0:T(128)S(1)}) all-reduce(f32[128]{0:T(128)S(1)} %get-tuple-element.150, f32[128]{0:T(128)S(1)} %get-tuple-element.149), channel_id=1, replica_groups=mesh['req'=16,'mp'=16] {'mp'}, use_global_device_ids=true, to_apply=%region_16.17 | all-reduce | flops 256 | bytes 2048 | tf_op jit(solution)/shard_map/psum | solution.py:179
  286.5 27.3 %all_gather.7 = bf16[128,2048]{1,0:T(8,128)(2,1)S(1)} all-gather(bf16[128,128]{1,0:T(8,128)(2,1)S(1)} %fusion.37), channel_id=1, replica_groups=mesh['req'=16,'mp'=16] {'mp'}, dimensions={1}, use_global_device_ids=true | all-gather | bytes 557056 | tf_op jit(solution)/shard_map/all_gather | solution.py:190
  316.6 77.9 %reduce-scatter.9.cloned.1.call-done = bf16[128,128]{1,0:T(8,128)(2,1)} async-done(((bf16[2048,128]{1,0:T(8,128)(2,1)}), bf16[128,128]{1,0:T(8,128)(2,1)}) %reduce-scatter.9.cloned.1.call-update) | async-done | bytes 32784
  (220 shorter events, 93.4 us)
Async XLA Ops:
  6.5 307.2 %copy-start = (bf16[2048,2,352]{0,2,1:T(8,128)(2,1)S(1)}, bf16[2048,2,352]{0,2,1:T(8,128)(2,1)}, u32[]{:S(2)}) copy-start(bf16[2048,2,352]{0,2,1:T(8,128)(2,1)} %param.20) | copy-start | bytes 8650756
  6.5 57.1 %all-gather.2.cloned.1.call-start = ((), (), s32[]{:S(2)}) async-start(), calls=%async_computation.2 | async-start | bytes 4456448 | tf_op jit(solution)/shard_map/all_gather | solution.py:156
  8.5 243.5 %reduce-scatter.7.cloned.1.call-start = ((), (), s32[]{:S(2)}) async-start(), calls=%async_computation.3 | async-start | bytes 557056
  8.6 9.8 %collective-permute-start = (bf16[128,128]{1,0:T(8,128)(2,1)}, bf16[128,128]{1,0:T(8,128)(2,1)S(1)}, u32[]{:S(2)}, u32[]{:S(2)}) collective-permute-start(bf16[128,128]{1,0:T(8,128)(2,1)} %param.12), channel_id=1, source_target_pairs={{0,1},{1,2},{2,3},{3,4},{4,5},{5,6},{6,7},{7,8},{8,9},{9,10},{10,1... | collective-permute-start | bytes 98312 | tf_op jit(solution)/shard_map/ppermute | solution.py:129
  10.2 8.3 %collective-permute-start.1 = (bf16[128,128]{1,0:T(8,128)(2,1)}, bf16[128,128]{1,0:T(8,128)(2,1)S(1)}, u32[]{:S(2)}, u32[]{:S(2)}) collective-permute-start(bf16[128,128]{1,0:T(8,128)(2,1)} %param.12), channel_id=1, source_target_pairs={{0,15},{1,0},{2,1},{3,2},{4,3},{5,4},{6,5},{7,6},{8,7},{9,8},{10,9... | collective-permute-start | bytes 98312 | tf_op jit(solution)/shard_map/ppermute | solution.py:134
  15.8 2.6 copy-start.4
  18.4 42.8 %copy-start.1 = (bf16[2048,3,128]{0,2,1:T(8,128)(2,1)S(1)}, bf16[2048,3,128]{0,2,1:T(8,128)(2,1)}, u32[]{:S(2)}) copy-start(bf16[2048,3,128]{0,2,1:T(8,128)(2,1)} %copy.29) | copy-start | bytes 4718596
  18.4 6.1 %collective-permute-start.2 = (bf16[128,128]{1,0:T(8,128)(2,1)S(1)}, bf16[128,128]{1,0:T(8,128)(2,1)S(1)}, u32[]{:S(2)}, u32[]{:S(2)}) collective-permute-start(bf16[128,128]{1,0:T(8,128)(2,1)S(1)} %collective-permute-done), channel_id=1, source_target_pairs={{0,1},{1,2},{2,3},{3,4},{4,5},{5,6},{6,7},{7,8},{8,9},{9,10},{10,1... | collective-permute-start | bytes 98312 | tf_op jit(solution)/shard_map/ppermute | solution.py:129
  18.5 6.0 %collective-permute-start.3 = (bf16[128,128]{1,0:T(8,128)(2,1)S(1)}, bf16[128,128]{1,0:T(8,128)(2,1)S(1)}, u32[]{:S(2)}, u32[]{:S(2)}) collective-permute-start(bf16[128,128]{1,0:T(8,128)(2,1)S(1)} %collective-permute-done.1), channel_id=1, source_target_pairs={{0,15},{1,0},{2,1},{3,2},{4,3},{5,4},{6,5},{7,6},{8,7},{9,8},{10,9... | collective-permute-start | bytes 98312 | tf_op jit(solution)/shard_map/ppermute | solution.py:134
  24.5 6.0 %collective-permute-start.4 = (bf16[128,128]{1,0:T(8,128)(2,1)S(1)}, bf16[128,128]{1,0:T(8,128)(2,1)S(1)}, u32[]{:S(2)}, u32[]{:S(2)}) collective-permute-start(bf16[128,128]{1,0:T(8,128)(2,1)S(1)} %collective-permute-done.2), channel_id=1, source_target_pairs={{0,1},{1,2},{2,3},{3,4},{4,5},{5,6},{6,7},{7,8},{8,9},{9,10},{10,1... | collective-permute-start | bytes 98312 | tf_op jit(solution)/shard_map/ppermute | solution.py:129
  24.5 6.0 %collective-permute-start.5 = (bf16[128,128]{1,0:T(8,128)(2,1)S(1)}, bf16[128,128]{1,0:T(8,128)(2,1)S(1)}, u32[]{:S(2)}, u32[]{:S(2)}) collective-permute-start(bf16[128,128]{1,0:T(8,128)(2,1)S(1)} %collective-permute-done.3), channel_id=1, source_target_pairs={{0,15},{1,0},{2,1},{3,2},{4,3},{5,4},{6,5},{7,6},{8,7},{9,8},{10,9... | collective-permute-start | bytes 98312 | tf_op jit(solution)/shard_map/ppermute | solution.py:134
  30.6 6.0 %collective-permute-start.6 = (bf16[128,128]{1,0:T(8,128)(2,1)S(1)}, bf16[128,128]{1,0:T(8,128)(2,1)S(1)}, u32[]{:S(2)}, u32[]{:S(2)}) collective-permute-start(bf16[128,128]{1,0:T(8,128)(2,1)S(1)} %collective-permute-done.4), channel_id=1, source_target_pairs={{0,1},{1,2},{2,3},{3,4},{4,5},{5,6},{6,7},{7,8},{8,9},{9,10},{10,1... | collective-permute-start | bytes 98312 | tf_op jit(solution)/shard_map/ppermute | solution.py:129
  30.6 6.0 %collective-permute-start.7 = (bf16[128,128]{1,0:T(8,128)(2,1)S(1)}, bf16[128,128]{1,0:T(8,128)(2,1)S(1)}, u32[]{:S(2)}, u32[]{:S(2)}) collective-permute-start(bf16[128,128]{1,0:T(8,128)(2,1)S(1)} %collective-permute-done.5), channel_id=1, source_target_pairs={{0,15},{1,0},{2,1},{3,2},{4,3},{5,4},{6,5},{7,6},{8,7},{9,8},{10,9... | collective-permute-start | bytes 98312 | tf_op jit(solution)/shard_map/ppermute | solution.py:134
  36.6 6.1 %collective-permute-start.8 = (bf16[128,128]{1,0:T(8,128)(2,1)S(1)}, bf16[128,128]{1,0:T(8,128)(2,1)S(1)}, u32[]{:S(2)}, u32[]{:S(2)}) collective-permute-start(bf16[128,128]{1,0:T(8,128)(2,1)S(1)} %collective-permute-done.6), channel_id=1, source_target_pairs={{0,1},{1,2},{2,3},{3,4},{4,5},{5,6},{6,7},{7,8},{8,9},{9,10},{10,1... | collective-permute-start | bytes 98312 | tf_op jit(solution)/shard_map/ppermute | solution.py:129
  36.6 6.1 %collective-permute-start.9 = (bf16[128,128]{1,0:T(8,128)(2,1)S(1)}, bf16[128,128]{1,0:T(8,128)(2,1)S(1)}, u32[]{:S(2)}, u32[]{:S(2)}) collective-permute-start(bf16[128,128]{1,0:T(8,128)(2,1)S(1)} %collective-permute-done.7), channel_id=1, source_target_pairs={{0,15},{1,0},{2,1},{3,2},{4,3},{5,4},{6,5},{7,6},{8,7},{9,8},{10,9... | collective-permute-start | bytes 98312 | tf_op jit(solution)/shard_map/ppermute | solution.py:134
  42.7 6.0 %collective-permute-start.10 = (bf16[128,128]{1,0:T(8,128)(2,1)S(1)}, bf16[128,128]{1,0:T(8,128)(2,1)S(1)}, u32[]{:S(2)}, u32[]{:S(2)}) collective-permute-start(bf16[128,128]{1,0:T(8,128)(2,1)S(1)} %collective-permute-done.8), channel_id=1, source_target_pairs={{0,1},{1,2},{2,3},{3,4},{4,5},{5,6},{6,7},{7,8},{8,9},{9,10},{10,1... | collective-permute-start | bytes 98312 | tf_op jit(solution)/shard_map/ppermute | solution.py:129
  42.7 6.0 %collective-permute-start.11 = (bf16[128,128]{1,0:T(8,128)(2,1)S(1)}, bf16[128,128]{1,0:T(8,128)(2,1)S(1)}, u32[]{:S(2)}, u32[]{:S(2)}) collective-permute-start(bf16[128,128]{1,0:T(8,128)(2,1)S(1)} %collective-permute-done.9), channel_id=1, source_target_pairs={{0,15},{1,0},{2,1},{3,2},{4,3},{5,4},{6,5},{7,6},{8,7},{9,8},{10,9... | collective-permute-start | bytes 98312 | tf_op jit(solution)/shard_map/ppermute | solution.py:134
  48.7 6.0 %collective-permute-start.12 = (bf16[128,128]{1,0:T(8,128)(2,1)S(1)}, bf16[128,128]{1,0:T(8,128)(2,1)S(1)}, u32[]{:S(2)}, u32[]{:S(2)}) collective-permute-start(bf16[128,128]{1,0:T(8,128)(2,1)S(1)} %collective-permute-done.10), channel_id=1, source_target_pairs={{0,1},{1,2},{2,3},{3,4},{4,5},{5,6},{6,7},{7,8},{8,9},{9,10},{10,1... | collective-permute-start | bytes 98312 | tf_op jit(solution)/shard_map/ppermute | solution.py:129
  48.7 6.0 %collective-permute-start.13 = (bf16[128,128]{1,0:T(8,128)(2,1)S(1)}, bf16[128,128]{1,0:T(8,128)(2,1)S(1)}, u32[]{:S(2)}, u32[]{:S(2)}) collective-permute-start(bf16[128,128]{1,0:T(8,128)(2,1)S(1)} %collective-permute-done.11), channel_id=1, source_target_pairs={{0,15},{1,0},{2,1},{3,2},{4,3},{5,4},{6,5},{7,6},{8,7},{9,8},{10,9... | collective-permute-start | bytes 98312 | tf_op jit(solution)/shard_map/ppermute | solution.py:134
  54.7 6.0 %collective-permute-start.14 = (bf16[128,128]{1,0:T(8,128)(2,1)S(1)}, bf16[128,128]{1,0:T(8,128)(2,1)S(1)}, u32[]{:S(2)}, u32[]{:S(2)}) collective-permute-start(bf16[128,128]{1,0:T(8,128)(2,1)S(1)} %collective-permute-done.12), channel_id=1, source_target_pairs={{0,1},{1,2},{2,3},{3,4},{4,5},{5,6},{6,7},{7,8},{8,9},{9,10},{10,1... | collective-permute-start | bytes 98312 | tf_op jit(solution)/shard_map/ppermute | solution.py:129
  162.6 90.4 %copy-start.3 = (bf16[128,128]{1,0:T(8,128)(2,1)S(1)}, bf16[128,128]{1,0:T(8,128)(2,1)}, u32[]{:S(2)}) copy-start(bf16[128,128]{1,0:T(8,128)(2,1)} %param.12) | copy-start | bytes 98308
  165.8 228.7 %reduce-scatter.9.cloned.1.call-start = ((), (), s32[]{:S(2)}) async-start(), calls=%async_computation.4 | async-start | bytes 557056
  313.7 1.4 copy-start.2
Sparse Core Ops, SparseCore 0:
  9.1 51.8 all-gather.1
  165.9 86.0 reduce-scatter.6
  316.7 77.6 reduce-scatter.8
